TPU v7x, 512 devices: a whole 4x8x8 slice. The times are simulated.
512 devices in a mesh: elem: 32 (over y_lo, z), orb: 16 (over x, y_hi, core).
Axes of the slice: x: 4, y: 8 (y_hi: 2, y_lo: 4; y = y_hi * 4 + y_lo), z: 8, core: 2. Of those that a mesh axis runs over, the one named last changes fastest.
Arguments:
- orbitals: bfloat16 [24576, 4096], P('elem', 'orb')
- hamiltonian: bfloat16 [384, 7, 64, 64], P('elem'), may hold values from -0.25 to 0.25
- neighbours: int32 [384, 7], P('elem'), may hold values from 0 to 383, as said below
Outputs:
- updated: bfloat16 [24576, 4096], P('elem', 'orb')
Inputs may be any that keep to these rules, and one draw needn't show every extreme that they name: Elements form tiles of 12 consecutive indices, each tile a periodic 3 x 4 plane of elements in some order, tiles stacked periodically. An element's row lists itself, its two neighbours along each in-plane direction, then the element at the same place in the previous tile and in the next tile.
All inputs are finite; a program needn't handle non-finite values.
Results may differ from a plain program's by a relative error of at most 0.0062.
Values may be sent and summed in bfloat16 or wider, within the bound.
A program may use at most 64 MiB of HBM per device.

v0:
```python
import jax
import jax.numpy as jnp
from jax import lax
from jax.sharding import PartitionSpec as P


def extended_2(value, sides, width):
    for axis, dim in sides:
        peers, length = (lax.axis_size(axis), value.shape[dim])
        up = [(i, (i + 1) % peers) for i in range(peers)]
        down = [(j, i) for i, j in up]
        last = lax.slice_in_dim(value, length - width, length, axis=dim)
        initial = lax.slice_in_dim(value, 0, width, axis=dim)
        before = lax.ppermute(last, axis, up)
        after = lax.ppermute(initial, axis, down)
        value = jnp.concatenate([before, value, after], axis=dim)
    return value


def neighbour_product(hamiltonian, local_index, field):
    rows, width = field.shape
    elements = hamiltonian.shape[0]
    block_size = hamiltonian.shape[2]
    extended = extended_2(field, (("elem", 0),), rows)
    blocks = extended.reshape(3 * elements, block_size, width)
    picked = blocks[local_index]
    result = jnp.einsum("enab,enbc->eac", hamiltonian, picked, preferred_element_type=jnp.float32)
    return result.reshape(rows, width)


def local(orbitals, hamiltonian, neighbours):
    elements = hamiltonian.shape[0]
    tiles = lax.axis_size("elem")
    my_tile = lax.axis_index("elem")
    other_tile = neighbours // elements
    relative = (other_tile - my_tile + tiles) % tiles
    slot = jnp.where(relative == 0, 1, jnp.where(relative == 1, 2, 0)).astype(jnp.int32)
    local_index = slot * elements + neighbours % elements
    start_field = orbitals.astype(jnp.float32)
    first = neighbour_product(hamiltonian, local_index, orbitals)
    first_half = first.astype(jnp.bfloat16)
    second = 2.0 * neighbour_product(hamiltonian, local_index, first_half) - start_field
    second_half = second.astype(jnp.bfloat16)
    third = 2.0 * neighbour_product(hamiltonian, local_index, second_half) - first
    filtered = third.astype(jnp.bfloat16)
    rows_total = filtered.shape[0] * tiles
    columns = filtered.shape[1]
    groups = lax.axis_size("orb")
    my_group = lax.axis_index("orb")
    orbital_count = columns * groups
    panel = lax.all_gather(filtered, "orb", axis=1, tiled=True)
    partial_gram = lax.dot_general(
        panel, filtered, (((0,), (0,)), ((), ())), preferred_element_type=jnp.float32
    )
    gram_part = lax.psum_scatter(partial_gram, "elem", scatter_dimension=0, tiled=True)
    share = gram_part.shape[0]
    row_global = my_tile * share + lax.broadcasted_iota(jnp.int32, gram_part.shape, 0)
    col_global = my_group * columns + lax.broadcasted_iota(jnp.int32, gram_part.shape, 1)
    own_diagonal = jnp.sum(jnp.where(row_global == col_global, gram_part, 0.0))
    total = lax.psum(own_diagonal, ("elem", "orb"))
    level = total / (orbital_count * rows_total)
    scaled_part = (gram_part / (level * rows_total)).astype(jnp.bfloat16)
    scaled = lax.all_gather(scaled_part, "elem", axis=0, tiled=True)
    mixed = jnp.dot(panel, scaled, preferred_element_type=jnp.float32)
    result = (1.5 * filtered.astype(jnp.float32) - 0.5 * mixed) / jnp.sqrt(level)
    return result.astype(jnp.bfloat16)


def solution(mesh):
    return jax.shard_map(
        local,
        mesh=mesh,
        in_specs=(P("elem", "orb"), P("elem", None, None, None), P("elem", None)),
        out_specs=P("elem", "orb"),
        check_vma=False,
    )
```

profile of v0, /device:TPU:6, one launch (start us, length us, event | category | flops | bytes accessed | tf_op | source)
XLA Modules:
  0.0 612.7 jit_solution(15075717939295863914)
XLA Ops:
  6.5 0.0 copy-start
  6.5 0.0 all-gather.3.cloned.1.call-start
  6.5 4.4 collective-permute-start
  10.9 11.6 %collective-permute-start.1 = (bf16[768,256]{1,0:T(8,128)(2,1)}, bf16[768,256]{1,0:T(8,128)(2,1)S(1)}, u32[]{:S(2)}, u32[]{:S(2)}) collective-permute-start(bf16[768,256]{1,0:T(8,128)(2,1)} %param.3), channel_id=1, source_target_pairs={{16,0},{32,16},{48,32},{64,48},{80,64},{96,80},{112,96},{128,112},... | collective-permute-start | bytes 1179656 | tf_op jit(solution)/shard_map/ppermute | solution.py:15
  22.6 0.7 compare_select_fusion
  23.3 0.1 copy.5
  23.4 0.1 reshape.24
  23.5 6.5 %collective-permute-done = bf16[768,256]{1,0:T(8,128)(2,1)S(1)} collective-permute-done((bf16[768,256]{1,0:T(8,128)(2,1)}, bf16[768,256]{1,0:T(8,128)(2,1)S(1)}, u32[]{:S(2)}, u32[]{:S(2)}) %collective-permute-start) | collective-permute-done | bytes 393248 | tf_op jit(solution)/shard_map/ppermute | solution.py:14
  30.0 1.3 collective-permute-done.1
  31.3 1.1 pad_maximum_fusion
  32.3 2.4 gather_fusion
  34.8 0.0 copy-done
  34.8 2.4 fusion.13
  37.2 1.9 collective-permute-start.2
  39.1 8.2 %collective-permute-start.3 = (bf16[768,256]{1,0:T(8,128)(2,1)S(1)}, bf16[768,256]{1,0:T(8,128)(2,1)S(1)}, u32[]{:S(2)}, u32[]{:S(2)}) collective-permute-start(bf16[768,256]{1,0:T(8,128)(2,1)S(1)} %bitcast.52), channel_id=1, source_target_pairs={{16,0},{32,16},{48,32},{64,48},{80,64},{96,80},{112,96},{128,112},... | collective-permute-start | bytes 1179656 | tf_op jit(solution)/shard_map/ppermute | solution.py:15
  47.3 6.3 %collective-permute-done.2 = bf16[768,256]{1,0:T(8,128)(2,1)S(1)} collective-permute-done((bf16[768,256]{1,0:T(8,128)(2,1)S(1)}, bf16[768,256]{1,0:T(8,128)(2,1)S(1)}, u32[]{:S(2)}, u32[]{:S(2)}) %collective-permute-start.2) | collective-permute-done | bytes 393248 | tf_op jit(solution)/shard_map/ppermute | solution.py:14
  53.6 1.2 collective-permute-done.3
  54.8 0.1 pad_maximum_fusion.1
  54.9 2.4 gather_fusion.1
  57.3 0.0 copy-start.1
  57.3 2.4 fusion.2
  59.8 0.0 copy-done.1
  59.8 0.1 fusion.7
  59.9 1.9 collective-permute-start.4
  61.8 8.3 %collective-permute-start.5 = (bf16[768,256]{1,0:T(8,128)(2,1)S(1)}, bf16[768,256]{1,0:T(8,128)(2,1)S(1)}, u32[]{:S(2)}, u32[]{:S(2)}) collective-permute-start(bf16[768,256]{1,0:T(8,128)(2,1)S(1)} %fusion.7), channel_id=1, source_target_pairs={{16,0},{32,16},{48,32},{64,48},{80,64},{96,80},{112,96},{128,112},... | collective-permute-start | bytes 1179656 | tf_op jit(solution)/shard_map/ppermute | solution.py:15
  70.1 5.5 collective-permute-done.4
  75.6 1.2 collective-permute-done.5
  76.7 0.1 pad_maximum_fusion.2
  76.8 2.4 gather_fusion.2
  79.3 3.1 fusion.4
  82.4 0.0 all-gather.3.cloned.1.call-update
  82.4 0.0 reduce-scatter.2.cloned.1.call-start
  82.4 91.2 %all-gather.3.cloned.1.call-done = bf16[768,4096]{1,0:T(8,128)(2,1)} async-done(((bf16[768,256]{1,0:T(8,128)(2,1)}), bf16[768,4096]{1,0:T(8,128)(2,1)}) %all-gather.3.cloned.1.call-update) | async-done | bytes 6291472 | tf_op jit(solution)/shard_map/all_gather | solution.py:51
  173.7 6.7 %fusion.14 = f32[4096,256]{1,0:T(8,128)} fusion(bf16[768,4096]{1,0:T(8,128)(2,1)} %all-gather.3.cloned.1.call-done, bf16[768,256]{1,0:T(8,128)(2,1)} %bitcast.55), kind=kOutput, calls=%fused_computation.37 | convolution fusion | flops 1610612736 | bytes 10878976 | tf_op jit(solution)/shard_map/dot_general | solution.py:52
  180.3 0.0 copy-start.2
  180.3 0.0 reduce-scatter.2.cloned.1.call-update
  180.4 0.0 all-gather.5.cloned.1.call-start
  180.4 172.7 %reduce-scatter.2.cloned.1.call-done = f32[128,256]{1,0:T(8,128)} async-done(((f32[4096,256]{1,0:T(8,128)}), f32[128,256]{1,0:T(8,128)}) %reduce-scatter.2.cloned.1.call-update) | async-done | bytes 131088 | tf_op jit(solution)/shard_map/reduce_scatter | solution.py:55
  353.2 1.6 select_reduce_fusion
  354.8 92.4 %psum.7 = f32[]{:T(128)} all-reduce(f32[]{:T(128)} %select_reduce_fusion), channel_id=1, replica_groups=mesh['elem'=32,'orb'=16] {'elem','orb'}, use_global_device_ids=true, to_apply=%region_2.3 | all-reduce | flops 1 | bytes 8 | tf_op jit(solution)/shard_map/psum | solution.py:60
  447.8 1.5 divide_convert_fusion
  449.3 0.0 all-gather.5.cloned.1.call-update
  450.0 150.2 %all-gather.5.cloned.1.call-done = bf16[4096,256]{1,0:T(8,128)(2,1)} async-done(((bf16[128,256]{1,0:T(8,128)(2,1)}), bf16[4096,256]{1,0:T(8,128)(2,1)}) %all-gather.5.cloned.1.call-update) | async-done | bytes 2097168 | tf_op jit(solution)/shard_map/all_gather | solution.py:63
  600.2 0.0 copy-done.2
  600.2 6.0 fusion.6
  (3 shorter events, 0.0 us)
Async XLA Ops:
  6.5 28.2 %copy-start = (bf16[12,7,64,64]{3,2,1,0:T(8,128)(2,1)S(1)}, bf16[12,7,64,64]{3,2,1,0:T(8,128)(2,1)}, u32[]{:S(2)}) copy-start(bf16[12,7,64,64]{3,2,1,0:T(8,128)(2,1)} %param.4) | copy-start | bytes 2064388
  6.5 167.1 %all-gather.3.cloned.1.call-start = ((), (), s32[]{:S(2)}) async-start(), calls=%async_computation.1 | async-start | bytes 6684672 | tf_op jit(solution)/shard_map/all_gather | solution.py:51
  6.5 23.4 %collective-permute-start = (bf16[768,256]{1,0:T(8,128)(2,1)}, bf16[768,256]{1,0:T(8,128)(2,1)S(1)}, u32[]{:S(2)}, u32[]{:S(2)}) collective-permute-start(bf16[768,256]{1,0:T(8,128)(2,1)} %param.3), channel_id=1, source_target_pairs={{0,16},{16,32},{32,48},{48,64},{64,80},{80,96},{96,112},{112,128},... | collective-permute-start | bytes 1179656 | tf_op jit(solution)/shard_map/ppermute | solution.py:14
  10.9 20.3 %collective-permute-start.1 = (bf16[768,256]{1,0:T(8,128)(2,1)}, bf16[768,256]{1,0:T(8,128)(2,1)S(1)}, u32[]{:S(2)}, u32[]{:S(2)}) collective-permute-start(bf16[768,256]{1,0:T(8,128)(2,1)} %param.3), channel_id=1, source_target_pairs={{16,0},{32,16},{48,32},{64,48},{80,64},{96,80},{112,96},{128,112},... | collective-permute-start | bytes 1179656 | tf_op jit(solution)/shard_map/ppermute | solution.py:15
  37.2 16.4 %collective-permute-start.2 = (bf16[768,256]{1,0:T(8,128)(2,1)S(1)}, bf16[768,256]{1,0:T(8,128)(2,1)S(1)}, u32[]{:S(2)}, u32[]{:S(2)}) collective-permute-start(bf16[768,256]{1,0:T(8,128)(2,1)S(1)} %bitcast.51), channel_id=1, source_target_pairs={{0,16},{16,32},{32,48},{48,64},{64,80},{80,96},{96,112},{112,128},... | collective-permute-start | bytes 1179656 | tf_op jit(solution)/shard_map/ppermute | solution.py:14
  39.1 15.7 %collective-permute-start.3 = (bf16[768,256]{1,0:T(8,128)(2,1)S(1)}, bf16[768,256]{1,0:T(8,128)(2,1)S(1)}, u32[]{:S(2)}, u32[]{:S(2)}) collective-permute-start(bf16[768,256]{1,0:T(8,128)(2,1)S(1)} %bitcast.52), channel_id=1, source_target_pairs={{16,0},{32,16},{48,32},{64,48},{80,64},{96,80},{112,96},{128,112},... | collective-permute-start | bytes 1179656 | tf_op jit(solution)/shard_map/ppermute | solution.py:15
  57.3 2.4 copy-start.1
  59.9 15.7 %collective-permute-start.4 = (bf16[768,256]{1,0:T(8,128)(2,1)S(1)}, bf16[768,256]{1,0:T(8,128)(2,1)S(1)}, u32[]{:S(2)}, u32[]{:S(2)}) collective-permute-start(bf16[768,256]{1,0:T(8,128)(2,1)S(1)} %fusion.7), channel_id=1, source_target_pairs={{0,16},{16,32},{32,48},{48,64},{64,80},{80,96},{96,112},{112,128},... | collective-permute-start | bytes 1179656 | tf_op jit(solution)/shard_map/ppermute | solution.py:14
  61.8 14.9 %collective-permute-start.5 = (bf16[768,256]{1,0:T(8,128)(2,1)S(1)}, bf16[768,256]{1,0:T(8,128)(2,1)S(1)}, u32[]{:S(2)}, u32[]{:S(2)}) collective-permute-start(bf16[768,256]{1,0:T(8,128)(2,1)S(1)} %fusion.7), channel_id=1, source_target_pairs={{16,0},{32,16},{48,32},{64,48},{80,64},{96,80},{112,96},{128,112},... | collective-permute-start | bytes 1179656 | tf_op jit(solution)/shard_map/ppermute | solution.py:15
  82.4 270.8 %reduce-scatter.2.cloned.1.call-start = ((), (), s32[]{:S(2)}) async-start(), calls=%async_computation.2 | async-start | bytes 4325376 | tf_op jit(solution)/shard_map/reduce_scatter | solution.py:55
  180.3 419.9 %copy-start.2 = (bf16[12,256,64]{1,2,0:T(8,128)(2,1)S(1)}, bf16[12,256,64]{1,2,0:T(8,128)(2,1)}, u32[]{:S(2)}) copy-start(bf16[12,256,64]{1,2,0:T(8,128)(2,1)} %fusion.4) | copy-start | bytes 1179652
  180.4 419.8 %all-gather.5.cloned.1.call-start = ((), (), s32[]{:S(2)}) async-start(), calls=%async_computation.3 | async-start | bytes 2162688 | tf_op jit(solution)/shard_map/all_gather | solution.py:63
Sparse Core Ops, SparseCore 0:
  82.5 91.1 all-gather.2
  180.5 172.6 reduce-scatter.1
  449.5 150.6 all-gather.4
where the time goes:
time: 613 us
  waiting for transfers between devices  436 us (71%)
  blocking collectives  92.4 us (15%)
  starting transfers between devices  36.5 us (6%)
  matrix products  20.6 us (3%)
  between operations  14.4 us (2%)
  local copies, waits for them, and re-layouts  7.51 us (1%)
    reduce_scatter x1, waiting for transfers between devices, local(): lax.psum_scatter(partial_gram, 'elem', scatter_dimension=0, tiled=True)  173 us
    all_gather x1, waiting for transfers between devices, local(): scaled = lax.all_gather(scaled_part, 'elem', axis=0, tiled=True)  150 us
    psum x1, blocking collectives, local(): total = lax.psum(own_diagonal, ('elem', 'orb'))  92.4 us
    all_gather x1, waiting for transfers between devices, local(): panel = lax.all_gather(filtered, 'orb', axis=1, tiled=True)  91.2 us
    ppermute x3, starting transfers between devices, extended_2(): after = lax.ppermute(initial, axis, down)  28.1 us
    ppermute x3, waiting for transfers between devices, extended_2(): before = lax.ppermute(last, axis, up)  18.2 us
  transfers between devices with their start and end apart: 9, of which 9 were waited for; matrix products, arithmetic and copies ran while one was open for 0% of the time, Pallas kernels for 0%

commit v1 on v0

v1 whole, which is shorter than its diff:
```python
import jax
import jax.numpy as jnp
from jax import lax
from jax.experimental import pallas as pl
from jax.experimental.pallas import tpu as pltpu
from jax.sharding import PartitionSpec as P

MESH = pl.DeviceIdType.MESH
F32 = jnp.float32
BF16 = jnp.bfloat16
NX, NY, NZ = 4, 4, 8
TILE, BLOCK, WIDTH, HALF = 12, 64, 256, 128
ROWS = TILE * BLOCK
PIECE = ROWS // 2
SLOTS = 16
GROUPS = 4
STRIP = WIDTH // NZ
UNROLL = 4
N_SEND, N_RECV = 256, 256


def rem(a, b):
    return lax.rem(a, jnp.int32(b))


def div(a, b):
    return lax.div(a, jnp.int32(b))


def slot_of(dx, dy, dc):
    return (dx * 2 + dy) * 2 + dc


def kernel(total_rows, total_cols, *refs):
    v_ref, ham_ref, nb_ref, out_ref = refs[:4]
    halos = refs[4:16]
    (w1a, w1b, w2a, w2b, hown, hhalo, first, acc, panel, relay, ft, ssq, lz, ly, lx, lsum, lev,
     tpart, rs_in, rs_out, zsum, y_in, y_out, tfull, mixed, ssem, rsem) = refs[16:]
    w1, w2 = (w1a, w1b), (w2a, w2b)

    e = lax.axis_index("elem")
    o = lax.axis_index("orb")
    z, yl = rem(e, NZ), div(e, NZ)
    c, yh, x = rem(o, 2), rem(div(o, 2), 2), div(o, 4)
    y = yh * NY + yl
    xc = x * 2 + c

    def dev(x_, y_, z_, c_):
        return (rem(y_, NY) * NZ + z_, (x_ * 2 + div(y_, NY)) * 2 + c_)

    def zdev(j):
        return dev(x, y, rem(z + j, NZ), c)

    def ydev(j):
        return dev(x, rem(y + j, 2 * NY), z, c)

    def xdev(j):
        return dev(rem(x + j, NX), y, z, c)

    def xcdev(j):
        t = rem(xc + j, 2 * NX)
        return dev(div(t, 2), y, z, rem(t, 2))

    sibling = dev(x, y, z, 1 - c)
    tile_next = (rem(e + 1, NZ * NY), o)
    tile_prev = (rem(e + NZ * NY - 1, NZ * NY), o)

    counts = [0, 0]
    finals = []

    def ids(n=1):
        s = counts[0]
        counts[0] += n
        assert counts[0] <= N_SEND
        return s

    def copy(src, dst, send_id, recv_id, to):
        return pltpu.make_async_remote_copy(
            src_ref=src, dst_ref=dst, send_sem=ssem.at[send_id], recv_sem=rsem.at[recv_id],
            device_id=to, device_id_type=MESH)

    def push(src, dst, cid, to):
        d = copy(src, dst, cid, cid, to)
        d.start()
        finals.append(d.wait_send)

    def arrived(dst, cid):
        copy(dst, dst, cid, cid, sibling).wait_recv()

    events = []

    def at(time, fn):
        events.append((time, fn))

    barrier = pltpu.get_barrier_semaphore()
    peers = [tile_next, tile_prev]
    peers += [zdev(j) for j in range(1, NZ)]
    peers += [ydev(j) for j in range(1, 2 * NY)]
    peers += [xcdev(j) for j in range(1, 2 * NX)]
    for p in peers:
        pl.semaphore_signal(barrier, inc=1, device_id=p, device_id_type=MESH)
    pl.semaphore_wait(barrier, len(peers))

    def cols(h):
        return pl.ds(h * HALF, HALF)

    def halo(k, h, d):
        return halos[(k * 2 + h) * 2 + d]

    halo_id = [[[ids() for d in range(2)] for h in range(2)] for k in range(3)]

    def source(k, h):
        return v_ref.at[:, :, cols(h)] if k == 0 else (w1[h] if k == 1 else w2[h])

    def send_halo(k, h):
        push(source(k, h), halo(k, h, 0), halo_id[k][h][0], tile_next)
        push(source(k, h), halo(k, h, 1), halo_id[k][h][1], tile_prev)

    def loop(body):
        def step(t, carry):
            for u in range(UNROLL):
                body(t * UNROLL + u)
            return carry
        lax.fori_loop(0, TILE // UNROLL, step, 0)

    def block_of(i, n):
        return rem(nb_ref[i, n], TILE)

    def setup(i):
        hown[i] = jnp.concatenate([ham_ref[i, n] for n in range(5)], axis=1)
        hhalo[i] = jnp.concatenate([ham_ref[i, n] for n in range(5, 7)], axis=1)

    def own_part(k, h):
        def body(i):
            if k == 0:
                parts = [v_ref[block_of(i, n), :, cols(h)] for n in range(5)]
            else:
                parts = [(w1, w2)[k - 1][h][block_of(i, n)] for n in range(5)]
            acc[h, i] = jnp.dot(hown[i], jnp.concatenate(parts, axis=0), preferred_element_type=F32)
        loop(body)

    def finish(k, h):
        for d in range(2):
            arrived(halo(k, h, d), halo_id[k][h][d])

        def body(i):
            parts = [halo(k, h, d)[block_of(i, 5 + d)] for d in range(2)]
            t = acc[h, i] + jnp.dot(hhalo[i], jnp.concatenate(parts, axis=0), preferred_element_type=F32)
            if k == 0:
                first[h, i] = t
                w1[h][i] = t.astype(BF16)
            elif k == 1:
                w2[h][i] = (2.0 * t - v_ref[i, :, cols(h)].astype(F32)).astype(BF16)
            else:
                f = (2.0 * t - first[h, i]).astype(BF16)
                panel[0, pl.ds(pl.multiple_of(i * BLOCK, BLOCK), BLOCK), cols(h)] = f
                f = f.astype(F32)
                ssq[...] += jnp.sum((f * f).reshape(BLOCK // 8, 8, HALF), axis=0)
        loop(body)

    def piece(q, h, r):
        return panel.at[q, pl.ds(r * PIECE, PIECE), cols(h)]

    def half(q, h):
        return panel.at[q, :, cols(h)]

    pid = {}

    def pids(*key):
        if key not in pid:
            pid[key] = ids()
        return pid[key]

    def to_sibling(dx, dy, h):
        push(half(slot_of(dx, dy, 0), h), half(slot_of(dx, dy, 1), h), pids("s", dx, dy, h), sibling)

    def from_sibling(dx, dy, h):
        arrived(half(slot_of(dx, dy, 1), h), pids("s", dx, dy, h))

    def x_send(dy, h):
        for r in range(2):
            push(piece(slot_of(0, dy, 0), h, r), piece(slot_of(3, dy, 0), h, r), pids("x", 3, dy, h, r), xdev(1))
            push(piece(slot_of(0, dy, 0), h, r), piece(slot_of(1, dy, 0), h, r), pids("x", 1, dy, h, r), xdev(NX - 1))

    def x_relay(dy, h):
        arrived(piece(slot_of(3, dy, 0), h, 0), pids("x", 3, dy, h, 0))
        push(piece(slot_of(3, dy, 0), h, 0), piece(slot_of(2, dy, 0), h, 0), pids("x", 2, dy, h, 0), xdev(1))
        arrived(piece(slot_of(1, dy, 0), h, 0), pids("x", 1, dy, h, 0))
        arrived(piece(slot_of(1, dy, 0), h, 1), pids("x", 1, dy, h, 1))
        push(piece(slot_of(1, dy, 0), h, 1), piece(slot_of(2, dy, 0), h, 1), pids("x", 2, dy, h, 1), xdev(NX - 1))
        arrived(piece(slot_of(3, dy, 0), h, 1), pids("x", 3, dy, h, 1))
        to_sibling(1, dy, h)
        to_sibling(3, dy, h)

    def x_far(dy, h):
        for r in range(2):
            arrived(piece(slot_of(2, dy, 0), h, r), pids("x", 2, dy, h, r))
        to_sibling(2, dy, h)

    def y_send(h):
        for r, j in ((0, 2), (1, 2 * NY - 2)):
            push(piece(0, h, r), relay.at[h, r], pids("y", h, r), ydev(j))

    def y_relay(h):
        for r, j in ((0, 2), (1, 2 * NY - 2)):
            arrived(relay.at[h, r], pids("y", h, r))
            push(relay.at[h, r], piece(slot_of(0, 1, 0), h, r), pids("Y", h, r), ydev(j))

    def partner(h):
        for r in range(2):
            arrived(piece(slot_of(0, 1, 0), h, r), pids("Y", h, r))
        x_send(1, h)
        to_sibling(0, 1, h)

    lev_id = [[ids() for j in range(8)] for s in range(3)]
    stages = ((lz, z, zdev), (ly, y, ydev), (lx, xc, xcdev))

    def level_send(s):
        buf, me, to = stages[s]
        if s:
            prev, prev_me, _ = stages[s - 1]
            for j in range(1, 8):
                arrived(prev.at[rem(prev_me + 8 - j, 8)], lev_id[s - 1][j])
            value = jnp.sum(prev[...], axis=0)
        else:
            value = ssq[...]
        lsum[s] = value
        buf[me] = value
        for j in range(1, 8):
            push(lsum.at[s], buf.at[me], lev_id[s][j], to(j))

    def level_done():
        for j in range(1, 8):
            arrived(lx.at[rem(xc + 8 - j, 8)], lev_id[2][j])
        total = jnp.sum(jnp.sum(lx[...], axis=0))
        level = jnp.full((8, HALF), total) / (total_cols * total_rows)
        lev[0] = level * total_rows
        lev[1] = jnp.sqrt(level)

    members = (
        ((0, 0), (1, 0)),
        ((3, 0), (2, 0)),
        ((0, 1), (1, 1)),
        ((3, 1), (2, 1)),
    )

    def slots(g):
        return [slot_of(dx, dy, dc) for dx, dy in members[g] for dc in range(2)]

    def hops(g):
        return (3, 4) if g % 2 == 0 else (4, 3)

    def strip(d):
        return pl.ds(pl.multiple_of(d * STRIP, STRIP), STRIP)

    def quad(g):
        return pl.ds(g * 4, 4)

    rs_id = [[[ids() for s in range(5)] for d in range(2)] for g in range(GROUPS)]
    ag_id = [[[ids() for s in range(5)] for d in range(2)] for g in range(GROUPS)]
    yr_id = ids(3)
    ys_id = [ids() for g in range(GROUPS)]
    yb_id = [ids() for g in range(GROUPS)]
    yb_send = [ids() for j in range(3)]

    def gram(g):
        for dx, dy in members[g]:
            for h in range(2):
                from_sibling(dx, dy, h)
        for n, q in enumerate(slots(g)):
            tpart[4 * g + n] = jnp.dot(ft[...], panel[q], preferred_element_type=F32)

    def rs_step(g, d, s):
        n = hops(g)[d]
        if s > n:
            return
        ahead = n - s + 1
        dest = rem(z + (ahead if d == 0 else NZ - ahead), NZ)
        value = tpart[quad(g), strip(dest), :]
        if s > 1:
            arrived(rs_in.at[g, d, s - 2], rs_id[g][d][s - 1])
            value = value + rs_in[g, d, s - 2].astype(F32)
        rs_out[g, d, s - 1] = value.astype(BF16)
        push(rs_out.at[g, d, s - 1], rs_in.at[g, d, s - 1], rs_id[g][d][s], zdev(1 if d == 0 else NZ - 1))

    def rs_done(g):
        value = tpart[quad(g), strip(z), :]
        for d in range(2):
            n = hops(g)[d]
            arrived(rs_in.at[g, d, n - 1], rs_id[g][d][n])
            value = value + rs_in[g, d, n - 1].astype(F32)
        zsum[g] = value
        slot = rem(yl + NY - g, NY) - 1
        slot = jnp.maximum(slot, 0)

        @pl.when(yl != g)
        def _():
            y_out[g] = value.astype(BF16)
            copy(y_out.at[g], y_in.at[slot], ys_id[g], yr_id + slot, dev(x, yh * NY + g, z, c)).start()

        def last():
            @pl.when(yl != g)
            def _():
                copy(y_out.at[g], y_in.at[slot], ys_id[g], yr_id + slot, dev(x, yh * NY + g, z, c)).wait_send()
        finals.append(last)

    def region(g, d):
        return tfull.at[quad(g), strip(d), :]

    def y_dest(g, j):
        return dev(x, yh * NY + (g + j) % NY, z, c)

    def scaled(g):
        @pl.when(yl == g)
        def _():
            value = zsum[g]
            for j in range(3):
                copy(y_in.at[j], y_in.at[j], 0, yr_id + j, sibling).wait_recv()
                value = value + y_in[j].astype(F32)
            value = value / jnp.max(lev[0])
            tfull[quad(g), strip(z), :] = value.astype(BF16)
            for j in range(1, NY):
                copy(region(g, z), region(g, z), yb_send[j - 1], yb_id[g], y_dest(g, j)).start()

        @pl.when(yl != g)
        def _():
            arrived(region(g, z), yb_id[g])

        def last():
            @pl.when(yl == g)
            def _():
                for j in range(1, NY):
                    copy(region(g, z), region(g, z), yb_send[j - 1], yb_id[g], y_dest(g, j)).wait_send()
        finals.append(last)

    def ag_step(g, d, s):
        n = hops(g)[d]
        if s > n:
            return
        behind = rem(z + ((NZ - s + 1) if d == 0 else (s - 1)), NZ)
        if s > 1:
            arrived(region(g, behind), ag_id[g][d][s - 1])
        push(region(g, behind), region(g, behind), ag_id[g][d][s], zdev(1 if d == 0 else NZ - 1))

    def ag_done(g):
        for d in range(2):
            n = hops(g)[d]
            arrived(region(g, rem(z + (NZ - n if d == 0 else n), NZ)), ag_id[g][d][n])

    def mix(g):
        ag_done(g)

        def step(t, carry):
            rows = pl.ds(pl.multiple_of(t * 256, 256), 256)
            value = None
            for n, q in enumerate(slots(g)):
                term = lax.dot_general(
                    panel[q, rows, :], tfull[4 * g + n], (((1,), (1,)), ((), ())), preferred_element_type=F32)
                value = term if value is None else value + term
            if g > 0:
                value = value + mixed[rows, :]
            if g < GROUPS - 1:
                mixed[rows, :] = value
            else:
                f = panel[0, rows, :].astype(F32)
                out_ref[rows, :] = ((1.5 * f - 0.5 * value) / jnp.max(lev[1])).astype(BF16)
            return carry
        lax.fori_loop(0, ROWS // 256, step, 0)

    def transposed(h):
        ft[pl.ds(h * HALF, HALF), :] = panel[0, :, cols(h)].T

    def launch(h):
        y_send(h)
        x_send(0, h)
        to_sibling(0, 0, h)
        transposed(h)

    send_halo(0, 0)
    send_halo(0, 1)
    ssq[...] = jnp.zeros_like(ssq)
    loop(setup)
    own_part(0, 0)
    own_part(0, 1)
    for k in range(3):
        for h in range(2):
            finish(k, h)
            if k < 2:
                send_halo(k + 1, h)
                own_part(k + 1, h)
            else:
                launch(h)

    at(0.5, lambda: level_send(0))
    at(5.0, lambda: level_send(1))
    at(9.5, lambda: level_send(2))
    at(14.0, level_done)
    for h in range(2):
        at((2.0, 6.3)[h], lambda h=h: x_relay(0, h))
        at((3.0, 7.2)[h], lambda h=h: y_relay(h))
        at((9.2, 15.0)[h], lambda h=h: partner(h))
        at((8.2, 10.5)[h], lambda h=h: x_far(0, h))
        at((15.1, 21.0)[h], lambda h=h: x_relay(1, h))
        at((18.0, 24.0)[h], lambda h=h: x_far(1, h))
    ready = (8.0, 12.5, 23.0, 26.0)
    for g in range(GROUPS):
        t0 = ready[g]
        at(t0, lambda g=g: gram(g))
        for s in range(1, 5):
            for d in range(2):
                at(t0 + 2.8 * (s - 1) + 0.01, lambda g=g, d=d, s=s: rs_step(g, d, s))
        t1 = t0 + 2.8 * 4
        at(t1, lambda g=g: rs_done(g))
        t2 = t1 + 3.0
        at(t2, lambda g=g: scaled(g))
        t3 = t2 + 1.5
        for s in range(1, 5):
            for d in range(2):
                at(t3 + 3.0 * (s - 1), lambda g=g, d=d, s=s: ag_step(g, d, s))
        at(t3 + 12.5, lambda g=g: mix(g))
    for _, fn in sorted(events, key=lambda item: item[0]):
        fn()
    for fn in finals:
        fn()


def solution(mesh):
    sizes = dict(mesh.shape)

    def local(orbitals, hamiltonian, neighbours):
        rows, width = orbitals.shape
        total_rows, total_cols = rows * sizes["elem"], width * sizes["orb"]
        assert (rows, width) == (ROWS, WIDTH)
        vmem = pl.BlockSpec(memory_space=pltpu.VMEM)
        block = pltpu.VMEM((TILE, BLOCK, HALF), BF16)
        return pl.pallas_call(
            lambda *refs: kernel(total_rows, total_cols, *refs),
            out_shape=jax.ShapeDtypeStruct((rows, width), BF16),
            in_specs=[vmem, vmem, pl.BlockSpec(memory_space=pltpu.SMEM)],
            out_specs=vmem,
            scratch_shapes=[block] * 16 + [
                pltpu.VMEM((TILE, BLOCK, 5 * BLOCK), BF16),
                pltpu.VMEM((TILE, BLOCK, 2 * BLOCK), BF16),
                pltpu.VMEM((2, TILE, BLOCK, HALF), F32),
                pltpu.VMEM((2, TILE, BLOCK, HALF), F32),
                pltpu.VMEM((SLOTS, ROWS, WIDTH), BF16),
                pltpu.VMEM((2, 2, PIECE, HALF), BF16),
                pltpu.VMEM((WIDTH, ROWS), BF16),
                pltpu.VMEM((8, HALF), F32),
                pltpu.VMEM((8, 8, HALF), F32),
                pltpu.VMEM((8, 8, HALF), F32),
                pltpu.VMEM((8, 8, HALF), F32),
                pltpu.VMEM((3, 8, HALF), F32),
                pltpu.VMEM((2, 8, HALF), F32),
                pltpu.VMEM((SLOTS, WIDTH, WIDTH), F32),
                pltpu.VMEM((GROUPS, 2, 4, 4, STRIP, WIDTH), BF16),
                pltpu.VMEM((GROUPS, 2, 4, 4, STRIP, WIDTH), BF16),
                pltpu.VMEM((GROUPS, 4, STRIP, WIDTH), F32),
                pltpu.VMEM((3, 4, STRIP, WIDTH), BF16),
                pltpu.VMEM((GROUPS, 4, STRIP, WIDTH), BF16),
                pltpu.VMEM((SLOTS, WIDTH, WIDTH), BF16),
                pltpu.VMEM((ROWS, WIDTH), F32),
                pltpu.SemaphoreType.DMA((N_SEND,)),
                pltpu.SemaphoreType.DMA((N_RECV,)),
            ],
            compiler_params=pltpu.CompilerParams(
                collective_id=0, has_side_effects=True, vmem_limit_bytes=56 * 1024 * 1024),
            name="filter_gram",
        )(orbitals.reshape(TILE, BLOCK, width), hamiltonian, neighbours)

    return jax.shard_map(
        local,
        mesh=mesh,
        in_specs=(P("elem", "orb"), P("elem", None, None, None), P("elem", None)),
        out_specs=P("elem", "orb"),
        check_vma=False,
    )
```

time: 613 us -> 147 us (0.24)
  waiting for transfers between devices: 436 us -> 0 us
  Pallas kernels: 0 us -> 142 us
  blocking collectives: 92.4 us -> 0 us
  starting transfers between devices: 36.5 us -> 0 us
  matrix products: 20.6 us -> 0 us
  between operations: 14.4 us -> 0.01 us
    all_gather x2 -> x0, waiting for transfers between devices: 241 us -> none  [the longest x1 150 us: local(): scaled = lax.all_gather(scaled_part, 'elem', axis=0, tiled=True)]
    reduce_scatter x1 -> x0, waiting for transfers between devices: 173 us -> none  [local(): lax.psum_scatter(partial_gram, 'elem', scatter_dimension=0, tiled=True)]
    pallas_call x0 -> x1, Pallas kernels: none -> 142 us  [local(): pl.pallas_call(lambda *refs: kernel(total_rows, total_cols, *refs), out_s...]
    psum x1 -> x0, blocking collectives: 92.4 us -> none  [local(): total = lax.psum(own_diagonal, ('elem', 'orb'))]
    ppermute x6 -> x0, starting transfers between devices: 36.4 us -> none  [the longest x3 28.1 us: extended_2(): after = lax.ppermute(initial, axis, down)]
    ppermute x6 -> x0, waiting for transfers between devices: 21.9 us -> none  [the longest x3 18.2 us: extended_2(): before = lax.ppermute(last, axis, up)]
    dot_general x5 -> x0, matrix products: 20.6 us -> none  [the longest x3 7.94 us: neighbour_product(): jnp.einsum('enab,enbc->eac', hamiltonian, picked, preferred_element_type=...]
    gather x3 -> x0, local copies, waits for them, and re-layouts: 7.32 us -> none  [neighbour_product(): picked = blocks[local_index]]
  transfers between devices with their start and end apart: 9 -> 0, of which waited for: 9 -> 0; matrix products, arithmetic and copies ran while one was open for 0% -> 0% of each run, Pallas kernels for 0% -> 0%
where the time goes in v1:
time: 147 us; the launch traced here: 145 us
  Pallas kernels  142 us (97%)
  local copies, waits for them, and re-layouts  3.13 us (2%)
    pallas_call x1, Pallas kernels, local(): pl.pallas_call(lambda *refs: kernel(total_rows, total_cols, *refs), out_s...  142 us
    unnamed x2, local copies, waits for them, and re-layouts  3.13 us

profile of v1, /device:TPU:6, one launch (start us, length us, event | category | flops | bytes accessed | tf_op | source)
XLA Modules:
  0.0 144.9 jit_solution(6003733869102575255)
XLA Ops:
  0.0 1.4 copy.4.refs_2_
  1.4 141.7 %filter_gram.1 = bf16[768,256]{1,0:T(8,128)(2,1)} custom-call(bf16[12,64,256]{2,1,0:T(8,128)(2,1)} %bitcast.1, bf16[12,7,64,64]{3,2,1,0:T(8,128)(2,1)} %refs_1_.1, s32[12,7]{1,0:T(8,128)} %copy.4.refs_2_), custom_call_target="tpu_custom_call" | custom-call | tf_op jit(solution)/shard_map/filter_gram/pallas_call | solution.py:436
  143.1 1.8 %copy.6 = bf16[768,256]{1,0:T(8,128)(2,1)} copy(bf16[768,256]{1,0:T(8,128)(2,1)} %filter_gram.1) | data formatting | bytes 786432

commit v2 on v1

v2 whole, which is shorter than its diff:
```python
import jax
import jax.numpy as jnp
from jax import lax
from jax.experimental import pallas as pl
from jax.experimental.pallas import tpu as pltpu
from jax.sharding import PartitionSpec as P

MESH = pl.DeviceIdType.MESH
F32 = jnp.float32
BF16 = jnp.bfloat16
NX, NY, NZ = 4, 4, 8
TILE, BLOCK, WIDTH, HALF = 12, 64, 256, 128
ROWS = TILE * BLOCK
PIECES = 4
PIECE = ROWS // PIECES
RIGHT, LEFT = (0, 1), (2, 3)
SLOTS = 16
GROUPS = 8
PAIR = 2
STRIP = WIDTH // NZ
UNROLL = 4
N_SEND, N_RECV = 256, 256
members = ((0, 0), (1, 0), (3, 0), (2, 0), (0, 1), (3, 1), (1, 1), (2, 1))
ORDER = (
    (4, 0, 0, 0), (0, 0), (2, 0, 0), (4, 0, 0, 1), (2, 0, 2), (5, 0, 0, 3), (5, 0, 0, 2), (7, 0), (8, 0, 1, 1),
    (8, 0, 0, 1), (6, 3, 0, 0), (2, 0, 3), (8, 0, 1, 2), (2, 0, 1), (5, 0, 1, 2), (6, 1, 0, 0), (2, 1, 0),
    (8, 0, 0, 2), (4, 0, 1, 0), (2, 1, 2), (4, 0, 1, 1), (0, 1), (6, 3, 0, 1), (5, 0, 1, 3), (6, 1, 0, 1), (2, 1, 1),
    (7, 2), (8, 2, 0, 1), (8, 2, 1, 1), (3, 0, 0), (6, 2, 0, 0), (3, 0, 2), (7, 1), (8, 1, 0, 1), (8, 1, 1, 1),
    (8, 0, 1, 3), (8, 0, 0, 3), (6, 2, 0, 1), (2, 1, 3), (3, 0, 1), (8, 2, 1, 2), (3, 0, 3), (8, 2, 0, 2), (7, 3),
    (4, 1, 0, 0), (8, 3, 0, 1), (8, 3, 1, 1), (5, 1, 0, 2), (8, 1, 1, 2), (8, 1, 0, 2), (3, 1, 0), (3, 1, 2),
    (6, 0, 1, 0), (8, 0, 1, 4), (5, 1, 0, 3), (6, 1, 1, 0), (8, 2, 1, 3), (4, 1, 0, 1), (8, 2, 0, 3), (8, 3, 0, 2),
    (3, 1, 1), (3, 1, 3), (6, 0, 1, 1), (6, 3, 1, 0), (8, 3, 1, 2), (0, 2), (8, 1, 1, 3), (8, 1, 0, 3), (4, 1, 1, 0),
    (9, 0), (7, 4), (8, 4, 0, 1), (8, 4, 1, 1), (8, 2, 1, 4), (5, 1, 1, 2), (8, 3, 0, 3), (8, 1, 0, 4), (4, 1, 1, 1),
    (5, 1, 1, 3), (6, 1, 1, 1), (8, 4, 0, 2), (8, 4, 1, 2), (6, 3, 1, 1), (8, 3, 1, 3), (9, 2), (8, 3, 0, 4),
    (6, 2, 1, 0), (7, 6), (8, 6, 0, 1), (8, 6, 1, 1), (9, 1), (1,), (7, 5), (8, 5, 1, 1), (8, 5, 0, 1), (6, 2, 1, 1),
    (8, 4, 1, 3), (8, 4, 0, 3), (10, 0), (7, 7), (8, 6, 1, 2), (8, 7, 1, 1), (8, 7, 0, 1), (8, 5, 0, 2), (8, 6, 0, 2),
    (8, 5, 1, 2), (9, 3), (8, 4, 1, 4), (11, 0, 1, 2), (11, 0, 0, 2), (8, 7, 0, 2), (8, 6, 1, 3), (10, 2),
    (8, 7, 1, 2), (8, 5, 0, 3), (9, 4), (8, 6, 0, 3), (10, 1), (8, 6, 1, 4), (8, 7, 0, 3), (8, 5, 1, 3),
    (11, 0, 1, 3), (10, 3), (8, 7, 1, 3), (11, 1, 1, 2), (8, 5, 0, 4), (11, 2, 1, 2), (11, 1, 0, 2), (9, 6),
    (8, 7, 0, 4), (11, 3, 0, 2), (10, 4), (11, 3, 1, 2), (11, 0, 0, 3), (11, 2, 0, 2), (9, 5), (11, 0, 1, 4),
    (11, 2, 1, 3), (11, 1, 0, 3), (11, 1, 1, 3), (11, 3, 0, 3), (9, 7), (11, 4, 1, 2), (10, 6), (11, 3, 1, 3),
    (11, 4, 0, 2), (11, 1, 0, 4), (11, 2, 1, 4), (11, 2, 0, 3), (11, 4, 1, 3), (10, 5), (11, 6, 0, 2), (12, 0),
    (11, 6, 1, 2), (10, 7), (11, 4, 1, 4), (11, 5, 0, 2), (11, 3, 0, 4), (11, 5, 1, 2), (11, 4, 0, 3), (12, 2),
    (11, 6, 1, 3), (11, 7, 0, 2), (11, 6, 0, 3), (11, 5, 0, 3), (11, 7, 1, 2), (12, 1), (11, 7, 0, 3), (11, 6, 1, 4),
    (11, 5, 1, 3), (12, 3), (11, 7, 1, 3), (11, 5, 0, 4), (11, 7, 0, 4), (12, 4), (12, 6), (12, 5), (12, 7),
)


def rem(a, b):
    return lax.rem(a, jnp.int32(b))


def div(a, b):
    return lax.div(a, jnp.int32(b))


def slot_of(dx, dy, dc):
    return (dx * 2 + dy) * 2 + dc


def kernel(total_rows, total_cols, *refs):
    v_in, ham_in, nb_ref, out_ref = refs[:4]
    halos = refs[4:16]
    (v_ref, ham_ref, w1a, w1b, w2a, w2b, hown, hhalo, first, acc, panel, relay, ft, ssq, lz, ly, lx, lsum, lev,
     tpart, rs_in, rs_out, zsum, y_in, y_out, tfull, mixed, ssem, rsem, lsem) = refs[16:]
    w1, w2 = (w1a, w1b), (w2a, w2b)

    e = lax.axis_index("elem")
    o = lax.axis_index("orb")
    z, yl = rem(e, NZ), div(e, NZ)
    c, yh, x = rem(o, 2), rem(div(o, 2), 2), div(o, 4)
    y = yh * NY + yl
    xc = x * 2 + c

    def dev(x_, y_, z_, c_):
        return (rem(y_, NY) * NZ + z_, (x_ * 2 + div(y_, NY)) * 2 + c_)

    def zdev(j):
        return dev(x, y, rem(z + j, NZ), c)

    def ydev(j):
        return dev(x, rem(y + j, 2 * NY), z, c)

    def xdev(j):
        return dev(rem(x + j, NX), y, z, c)

    def xcdev(j):
        t = rem(xc + j, 2 * NX)
        return dev(div(t, 2), y, z, rem(t, 2))

    sibling = dev(x, y, z, 1 - c)
    tile_next = (rem(e + 1, NZ * NY), o)
    tile_prev = (rem(e + NZ * NY - 1, NZ * NY), o)

    counts = [0, 0]
    finals = []

    def ids(n=1):
        s = counts[0]
        counts[0] += n
        assert counts[0] <= N_SEND
        return s

    def copy(src, dst, send_id, recv_id, to):
        return pltpu.make_async_remote_copy(
            src_ref=src, dst_ref=dst, send_sem=ssem.at[send_id], recv_sem=rsem.at[recv_id],
            device_id=to, device_id_type=MESH)

    def push(src, dst, cid, to):
        d = copy(src, dst, cid, cid, to)
        d.start()
        finals.append(d.wait_send)

    def arrived(dst, cid):
        copy(dst, dst, cid, cid, sibling).wait_recv()

    load_v = pltpu.make_async_copy(v_in, v_ref, lsem.at[0])
    load_ham = pltpu.make_async_copy(ham_in, ham_ref, lsem.at[1])
    load_v.start()
    load_ham.start()

    barrier = pltpu.get_barrier_semaphore()
    peers = [tile_next, tile_prev]
    peers += [zdev(j) for j in range(1, NZ)]
    peers += [ydev(j) for j in range(1, 2 * NY)]
    peers += [xcdev(j) for j in range(1, 2 * NX)]
    for p in peers:
        pl.semaphore_signal(barrier, inc=1, device_id=p, device_id_type=MESH)
    pl.semaphore_wait(barrier, len(peers))

    def cols(h):
        return pl.ds(h * HALF, HALF)

    def halo(k, h, d):
        return halos[(k * 2 + h) * 2 + d]

    halo_id = [[[ids() for d in range(2)] for h in range(2)] for k in range(3)]

    def source(k, h):
        return v_ref.at[:, :, cols(h)] if k == 0 else (w1[h] if k == 1 else w2[h])

    def send_halo(k, h):
        push(source(k, h), halo(k, h, 0), halo_id[k][h][0], tile_next)
        push(source(k, h), halo(k, h, 1), halo_id[k][h][1], tile_prev)

    def loop(body):
        def step(t, carry):
            for u in range(UNROLL):
                body(t * UNROLL + u)
            return carry
        lax.fori_loop(0, TILE // UNROLL, step, 0)

    def block_of(i, n):
        return rem(nb_ref[n, i], TILE)

    def setup(i):
        hown[i] = jnp.concatenate([ham_ref[i, n] for n in range(5)], axis=1)
        hhalo[i] = jnp.concatenate([ham_ref[i, n] for n in range(5, 7)], axis=1)

    def own_part(k, h):
        def body(i):
            if k == 0:
                parts = [v_ref[block_of(i, n), :, cols(h)] for n in range(5)]
            else:
                parts = [(w1, w2)[k - 1][h][block_of(i, n)] for n in range(5)]
            acc[h, i] = jnp.dot(hown[i], jnp.concatenate(parts, axis=0), preferred_element_type=F32)
        loop(body)

    def finish(k, h):
        for d in range(2):
            arrived(halo(k, h, d), halo_id[k][h][d])

        def body(i):
            parts = [halo(k, h, d)[block_of(i, 5 + d)] for d in range(2)]
            t = acc[h, i] + jnp.dot(hhalo[i], jnp.concatenate(parts, axis=0), preferred_element_type=F32)
            if k == 0:
                first[h, i] = t
                w1[h][i] = t.astype(BF16)
            elif k == 1:
                w2[h][i] = (2.0 * t - v_ref[i, :, cols(h)].astype(F32)).astype(BF16)
            else:
                f = (2.0 * t - first[h, i]).astype(BF16)
                panel[0, pl.ds(pl.multiple_of(i * BLOCK, BLOCK), BLOCK), cols(h)] = f
                f = f.astype(F32)
                ssq[...] += jnp.sum((f * f).reshape(BLOCK // 8, 8, HALF), axis=0)
        loop(body)

    def piece(q, h, r):
        return panel.at[q, pl.ds(r * PIECE, PIECE), cols(h)]

    def half(q, h):
        return panel.at[q, :, cols(h)]

    pid = {}

    def pids(*key):
        if key not in pid:
            pid[key] = ids()
        return pid[key]

    def to_sibling(dx, dy, h):
        push(half(slot_of(dx, dy, 0), h), half(slot_of(dx, dy, 1), h), pids("s", dx, dy, h), sibling)

    def from_sibling(dx, dy, h):
        arrived(half(slot_of(dx, dy, 1), h), pids("s", dx, dy, h))

    def x_send(dy, h, r):
        push(piece(slot_of(0, dy, 0), h, r), piece(slot_of(3, dy, 0), h, r), pids("x", 3, dy, h, r), xdev(1))
        push(piece(slot_of(0, dy, 0), h, r), piece(slot_of(1, dy, 0), h, r), pids("x", 1, dy, h, r), xdev(NX - 1))

    def y_step(r):
        return ydev(2 if r in RIGHT else 2 * NY - 2)

    def y_send(h):
        for r in (0, 2, 1, 3):
            push(piece(0, h, r), relay.at[h, r], pids("y", h, r), y_step(r))

    def do_yr(h, r):
        arrived(relay.at[h, r], pids("y", h, r))
        push(relay.at[h, r], piece(slot_of(0, 1, 0), h, r), pids("Y", h, r), y_step(r))

    def do_par(h, r):
        arrived(piece(slot_of(0, 1, 0), h, r), pids("Y", h, r))
        x_send(1, h, r)

    def do_f3(dy, h, r):
        arrived(piece(slot_of(3, dy, 0), h, r), pids("x", 3, dy, h, r))
        push(piece(slot_of(3, dy, 0), h, r), piece(slot_of(2, dy, 0), h, r), pids("x", 2, dy, h, r), xdev(1))

    def do_f1(dy, h, r):
        arrived(piece(slot_of(1, dy, 0), h, r), pids("x", 1, dy, h, r))
        push(piece(slot_of(1, dy, 0), h, r), piece(slot_of(2, dy, 0), h, r), pids("x", 2, dy, h, r), xdev(NX - 1))

    def do_sib(dx, dy, h):
        for r in ((), RIGHT, RIGHT + LEFT, LEFT)[dx]:
            arrived(piece(slot_of(dx, dy, 0), h, r), pids("x", dx, dy, h, r))
        to_sibling(dx, dy, h)

    lev_id = [[ids() for j in range(8)] for s in range(3)]
    stages = ((lz, z, zdev), (ly, y, ydev), (lx, xc, xcdev))

    def do_ls(s):
        buf, me, to = stages[s]
        if s:
            prev, prev_me, _ = stages[s - 1]
            for j in range(1, 8):
                arrived(prev.at[rem(prev_me + 8 - j, 8)], lev_id[s - 1][j])
            value = jnp.sum(prev[...], axis=0)
        else:
            value = ssq[...]
        lsum[s] = value
        buf[me] = value
        for j in range(1, 8):
            push(lsum.at[s], buf.at[me], lev_id[s][j], to(j))

    def do_ld():
        for j in range(1, 8):
            arrived(lx.at[rem(xc + 8 - j, 8)], lev_id[2][j])
        total = jnp.sum(jnp.sum(lx[...], axis=0))
        level = jnp.full((8, HALF), total) / (total_cols * total_rows)
        lev[0] = level * total_rows
        lev[1] = jnp.sqrt(level)

    def slots(g):
        return [slot_of(*members[g], dc) for dc in range(PAIR)]

    def hops(g):
        return (3, 4) if g % 2 == 0 else (4, 3)

    def strip(d):
        return pl.ds(pl.multiple_of(d * STRIP, STRIP), STRIP)

    def pair(g):
        return pl.ds(slots(g)[0], PAIR)

    rs_id = [[[ids() for s in range(hops(g)[d])] for d in range(2)] for g in range(GROUPS)]
    ag_id = [[[ids() for s in range(hops(g)[d])] for d in range(2)] for g in range(GROUPS)]
    y_id = [[ids() for j in range(NY - 1)] for g in range(GROUPS)]

    def along_z(d):
        return zdev(1 if d == 0 else NZ - 1)

    def do_gram(g):
        for h in range(2):
            from_sibling(*members[g], h)
        for q in slots(g):
            tpart[q] = jnp.dot(ft[...], panel[q], preferred_element_type=F32)

    def do_rs(g, d, s):
        ahead = hops(g)[d] - s + 1
        dest = rem(z + (ahead if d == 0 else NZ - ahead), NZ)
        value = tpart[pair(g), strip(dest), :]
        if s > 1:
            arrived(rs_in.at[g, d, s - 2], rs_id[g][d][s - 2])
            value = value + rs_in[g, d, s - 2].astype(F32)
        rs_out[g, d, s - 1] = value.astype(BF16)
        push(rs_out.at[g, d, s - 1], rs_in.at[g, d, s - 1], rs_id[g][d][s - 1], along_z(d))

    def do_rsd(g):
        value = tpart[pair(g), strip(z), :]
        for d in range(2):
            n = hops(g)[d]
            arrived(rs_in.at[g, d, n - 1], rs_id[g][d][n - 1])
            value = value + rs_in[g, d, n - 1].astype(F32)
        zsum[g] = value
        y_out[g] = value.astype(BF16)
        for j in range(1, NY):
            push(y_out.at[g], y_in.at[g, j - 1], y_id[g][j - 1], dev(x, yh * NY + rem(yl + j, NY), z, c))

    def region(g, d):
        return tfull.at[pair(g), strip(d), :]

    def ag_send(g, d, s):
        behind = rem(z + ((NZ - s + 1) if d == 0 else (s - 1)), NZ)
        if s > 1:
            arrived(region(g, behind), ag_id[g][d][s - 2])
        push(region(g, behind), region(g, behind), ag_id[g][d][s - 1], along_z(d))

    def do_sc(g):
        value = zsum[g]
        for j in range(NY - 1):
            arrived(y_in.at[g, j], y_id[g][j])
            value = value + y_in[g, j].astype(F32)
        value = value / jnp.max(lev[0])
        tfull[pair(g), strip(z), :] = value.astype(BF16)
        for d in range(2):
            ag_send(g, d, 1)

    do_ag = ag_send

    def do_mix(g):
        for d in range(2):
            n = hops(g)[d]
            arrived(region(g, rem(z + (NZ - n if d == 0 else n), NZ)), ag_id[g][d][n - 1])
        initial, final = g == mixes[0], g == mixes[-1]

        def step(t, carry):
            rows = pl.ds(pl.multiple_of(t * 256, 256), 256)
            value = None
            for q in slots(g):
                term = lax.dot_general(
                    panel[q, rows, :], tfull[q], (((1,), (1,)), ((), ())), preferred_element_type=F32)
                value = term if value is None else value + term
            if not initial:
                value = value + mixed[rows, :]
            if final:
                f = panel[0, rows, :].astype(F32)
                out_ref[rows, :] = ((1.5 * f - 0.5 * value) / jnp.max(lev[1])).astype(BF16)
            else:
                mixed[rows, :] = value
            return carry
        lax.fori_loop(0, ROWS // 256, step, 0)

    def transposed(h):
        ft[pl.ds(h * HALF, HALF), :] = panel[0, :, cols(h)].T

    def launch(h):
        y_send(h)
        for r in (0, 2, 1, 3):
            x_send(0, h, r)
        to_sibling(0, 0, h)
        transposed(h)

    load_v.wait()
    send_halo(0, 0)
    send_halo(0, 1)
    ssq[...] = jnp.zeros_like(ssq)
    load_ham.wait()
    loop(setup)
    own_part(0, 0)
    own_part(0, 1)
    for k in range(3):
        for h in range(2):
            finish(k, h)
            if k < 2:
                send_halo(k + 1, h)
                own_part(k + 1, h)
            else:
                launch(h)

    steps = (do_ls, do_ld, do_yr, do_par, do_f3, do_f1, do_sib, do_gram, do_rs, do_rsd, do_sc, do_ag, do_mix)
    mixes = [numbers[0] for kind, *numbers in ORDER if steps[kind] is do_mix]
    for kind, *numbers in ORDER:
        steps[kind](*numbers)
    for fn in finals:
        fn()


def solution(mesh):
    sizes = dict(mesh.shape)

    def local(orbitals, hamiltonian, neighbours):
        rows, width = orbitals.shape
        total_rows, total_cols = rows * sizes["elem"], width * sizes["orb"]
        assert (rows, width) == (ROWS, WIDTH)
        vmem = pl.BlockSpec(memory_space=pltpu.VMEM)
        anywhere = pl.BlockSpec(memory_space=pl.ANY)
        block = pltpu.VMEM((TILE, BLOCK, HALF), BF16)
        return pl.pallas_call(
            lambda *refs: kernel(total_rows, total_cols, *refs),
            out_shape=jax.ShapeDtypeStruct((rows, width), BF16),
            in_specs=[anywhere, anywhere, pl.BlockSpec(memory_space=pltpu.SMEM)],
            out_specs=vmem,
            scratch_shapes=[block] * 12 + [
                pltpu.VMEM((TILE, BLOCK, WIDTH), BF16),
                pltpu.VMEM(hamiltonian.shape, BF16),
            ] + [block] * 4 + [
                pltpu.VMEM((TILE, BLOCK, 5 * BLOCK), BF16),
                pltpu.VMEM((TILE, BLOCK, 2 * BLOCK), BF16),
                pltpu.VMEM((2, TILE, BLOCK, HALF), F32),
                pltpu.VMEM((2, TILE, BLOCK, HALF), F32),
                pltpu.VMEM((SLOTS, ROWS, WIDTH), BF16),
                pltpu.VMEM((2, PIECES, PIECE, HALF), BF16),
                pltpu.VMEM((WIDTH, ROWS), BF16),
                pltpu.VMEM((8, HALF), F32),
                pltpu.VMEM((8, 8, HALF), F32),
                pltpu.VMEM((8, 8, HALF), F32),
                pltpu.VMEM((8, 8, HALF), F32),
                pltpu.VMEM((3, 8, HALF), F32),
                pltpu.VMEM((2, 8, HALF), F32),
                pltpu.VMEM((SLOTS, WIDTH, WIDTH), F32),
                pltpu.VMEM((GROUPS, 2, 4, PAIR, STRIP, WIDTH), BF16),
                pltpu.VMEM((GROUPS, 2, 4, PAIR, STRIP, WIDTH), BF16),
                pltpu.VMEM((GROUPS, PAIR, STRIP, WIDTH), F32),
                pltpu.VMEM((GROUPS, NY - 1, PAIR, STRIP, WIDTH), BF16),
                pltpu.VMEM((GROUPS, PAIR, STRIP, WIDTH), BF16),
                pltpu.VMEM((SLOTS, WIDTH, WIDTH), BF16),
                pltpu.VMEM((ROWS, WIDTH), F32),
                pltpu.SemaphoreType.DMA((N_SEND,)),
                pltpu.SemaphoreType.DMA((N_RECV,)),
                pltpu.SemaphoreType.DMA((2,)),
            ],
            compiler_params=pltpu.CompilerParams(
                collective_id=0, has_side_effects=True, vmem_limit_bytes=56 * 1024 * 1024),
            name="filter_gram",
        )(orbitals.reshape(TILE, BLOCK, width), hamiltonian, neighbours.T)

    return jax.shard_map(
        local,
        mesh=mesh,
        in_specs=(P("elem", "orb"), P("elem", None, None, None), P("elem", None)),
        out_specs=P("elem", "orb"),
        check_vma=False,
    )
```

time: 147 us -> 117 us (0.80)
  Pallas kernels: 142 us -> 115 us
    pallas_call x1, Pallas kernels: 142 us -> 115 us  [local(): pl.pallas_call(lambda *refs: kernel(total_rows, total_cols, *refs), out_s...]
    unnamed x2 -> x1, local copies, waits for them, and re-layouts: 3.13 us -> 1.77 us
where the time goes in v2:
time: 117 us; the launch traced here: 116 us
  Pallas kernels  115 us (98%)
  local copies, waits for them, and re-layouts  1.77 us (2%)
    pallas_call x1, Pallas kernels, local(): pl.pallas_call(lambda *refs: kernel(total_rows, total_cols, *refs), out_s...  115 us

profile of v2, /device:TPU:6, one launch (start us, length us, event | category | flops | bytes accessed | tf_op | source)
XLA Modules:
  0.0 116.4 jit_solution(1011341768065068115)
XLA Ops:
  0.0 114.6 %filter_gram.1 = bf16[768,256]{1,0:T(8,128)(2,1)} custom-call(bf16[12,64,256]{2,1,0:T(8,128)(2,1)} %bitcast.2, bf16[12,7,64,64]{3,2,1,0:T(8,128)(2,1)} %refs_1_.1, s32[7,12]{1,0:T(8,128)} %bitcast.3), custom_call_target="tpu_custom_call" | custom-call | tf_op jit(solution)/shard_map/filter_gram/pallas_call | solution.py:399
  114.6 1.8 %copy.5 = bf16[768,256]{1,0:T(8,128)(2,1)} copy(bf16[768,256]{1,0:T(8,128)(2,1)} %filter_gram.1) | data formatting | bytes 786432

commit v3 on v2

--- a/solution.py
+++ b/solution.py
@@ -15,34 +15,34 @@
 PIECE = ROWS // PIECES
 RIGHT, LEFT = (0, 1), (2, 3)
 SLOTS = 16
-GROUPS = 8
+GROUPS, SUMMED = 8, 7
 PAIR = 2
 STRIP = WIDTH // NZ
 UNROLL = 4
+MIX_ROWS = 768
 N_SEND, N_RECV = 256, 256
-members = ((0, 0), (1, 0), (3, 0), (2, 0), (0, 1), (3, 1), (1, 1), (2, 1))
+members = ((1, 0), (0, 0), (2, 0), (0, 1), (3, 1), (1, 1), (2, 1), (3, 0))
 ORDER = (
-    (4, 0, 0, 0), (0, 0), (2, 0, 0), (4, 0, 0, 1), (2, 0, 2), (5, 0, 0, 3), (5, 0, 0, 2), (7, 0), (8, 0, 1, 1),
-    (8, 0, 0, 1), (6, 3, 0, 0), (2, 0, 3), (8, 0, 1, 2), (2, 0, 1), (5, 0, 1, 2), (6, 1, 0, 0), (2, 1, 0),
-    (8, 0, 0, 2), (4, 0, 1, 0), (2, 1, 2), (4, 0, 1, 1), (0, 1), (6, 3, 0, 1), (5, 0, 1, 3), (6, 1, 0, 1), (2, 1, 1),
-    (7, 2), (8, 2, 0, 1), (8, 2, 1, 1), (3, 0, 0), (6, 2, 0, 0), (3, 0, 2), (7, 1), (8, 1, 0, 1), (8, 1, 1, 1),
-    (8, 0, 1, 3), (8, 0, 0, 3), (6, 2, 0, 1), (2, 1, 3), (3, 0, 1), (8, 2, 1, 2), (3, 0, 3), (8, 2, 0, 2), (7, 3),
-    (4, 1, 0, 0), (8, 3, 0, 1), (8, 3, 1, 1), (5, 1, 0, 2), (8, 1, 1, 2), (8, 1, 0, 2), (3, 1, 0), (3, 1, 2),
-    (6, 0, 1, 0), (8, 0, 1, 4), (5, 1, 0, 3), (6, 1, 1, 0), (8, 2, 1, 3), (4, 1, 0, 1), (8, 2, 0, 3), (8, 3, 0, 2),
-    (3, 1, 1), (3, 1, 3), (6, 0, 1, 1), (6, 3, 1, 0), (8, 3, 1, 2), (0, 2), (8, 1, 1, 3), (8, 1, 0, 3), (4, 1, 1, 0),
-    (9, 0), (7, 4), (8, 4, 0, 1), (8, 4, 1, 1), (8, 2, 1, 4), (5, 1, 1, 2), (8, 3, 0, 3), (8, 1, 0, 4), (4, 1, 1, 1),
-    (5, 1, 1, 3), (6, 1, 1, 1), (8, 4, 0, 2), (8, 4, 1, 2), (6, 3, 1, 1), (8, 3, 1, 3), (9, 2), (8, 3, 0, 4),
-    (6, 2, 1, 0), (7, 6), (8, 6, 0, 1), (8, 6, 1, 1), (9, 1), (1,), (7, 5), (8, 5, 1, 1), (8, 5, 0, 1), (6, 2, 1, 1),
-    (8, 4, 1, 3), (8, 4, 0, 3), (10, 0), (7, 7), (8, 6, 1, 2), (8, 7, 1, 1), (8, 7, 0, 1), (8, 5, 0, 2), (8, 6, 0, 2),
-    (8, 5, 1, 2), (9, 3), (8, 4, 1, 4), (11, 0, 1, 2), (11, 0, 0, 2), (8, 7, 0, 2), (8, 6, 1, 3), (10, 2),
-    (8, 7, 1, 2), (8, 5, 0, 3), (9, 4), (8, 6, 0, 3), (10, 1), (8, 6, 1, 4), (8, 7, 0, 3), (8, 5, 1, 3),
-    (11, 0, 1, 3), (10, 3), (8, 7, 1, 3), (11, 1, 1, 2), (8, 5, 0, 4), (11, 2, 1, 2), (11, 1, 0, 2), (9, 6),
-    (8, 7, 0, 4), (11, 3, 0, 2), (10, 4), (11, 3, 1, 2), (11, 0, 0, 3), (11, 2, 0, 2), (9, 5), (11, 0, 1, 4),
-    (11, 2, 1, 3), (11, 1, 0, 3), (11, 1, 1, 3), (11, 3, 0, 3), (9, 7), (11, 4, 1, 2), (10, 6), (11, 3, 1, 3),
-    (11, 4, 0, 2), (11, 1, 0, 4), (11, 2, 1, 4), (11, 2, 0, 3), (11, 4, 1, 3), (10, 5), (11, 6, 0, 2), (12, 0),
-    (11, 6, 1, 2), (10, 7), (11, 4, 1, 4), (11, 5, 0, 2), (11, 3, 0, 4), (11, 5, 1, 2), (11, 4, 0, 3), (12, 2),
-    (11, 6, 1, 3), (11, 7, 0, 2), (11, 6, 0, 3), (11, 5, 0, 3), (11, 7, 1, 2), (12, 1), (11, 7, 0, 3), (11, 6, 1, 4),
-    (11, 5, 1, 3), (12, 3), (11, 7, 1, 3), (11, 5, 0, 4), (11, 7, 0, 4), (12, 4), (12, 6), (12, 5), (12, 7),
+    (0, 0), (7, 1), (4, 0, 0, 1), (8, 1, 0, 1), (5, 0, 0, 2), (5, 0, 0, 3), (4, 0, 0, 0), (2, 0, 0), (6, 1, 0, 0),
+    (6, 3, 0, 0), (2, 0, 2), (8, 1, 1, 1), (2, 0, 1), (2, 0, 3), (5, 0, 1, 2), (4, 0, 1, 0), (8, 1, 0, 2), (2, 1, 2),
+    (8, 1, 1, 2), (2, 1, 0), (5, 0, 1, 3), (4, 0, 1, 1), (6, 1, 0, 1), (2, 1, 1), (3, 0, 0), (6, 3, 0, 1), (2, 1, 3),
+    (6, 2, 0, 0), (7, 0), (8, 0, 1, 1), (8, 0, 0, 1), (3, 0, 2), (3, 0, 1), (8, 1, 0, 3), (6, 2, 0, 1), (0, 1),
+    (8, 1, 1, 3), (3, 0, 3), (8, 0, 0, 2), (8, 0, 1, 2), (6, 0, 1, 0), (5, 1, 0, 2), (4, 1, 0, 0), (7, 2),
+    (8, 2, 1, 1), (3, 1, 0), (8, 2, 0, 1), (3, 1, 2), (4, 1, 0, 1), (5, 1, 0, 3), (3, 1, 1), (6, 1, 1, 0),
+    (8, 1, 0, 4), (3, 1, 3), (6, 0, 1, 1), (8, 0, 1, 3), (6, 3, 1, 0), (8, 0, 0, 3), (8, 2, 1, 2), (8, 2, 0, 2),
+    (7, 3), (4, 1, 1, 0), (8, 3, 0, 1), (5, 1, 1, 2), (8, 3, 1, 1), (8, 2, 1, 3), (9, 1), (6, 2, 1, 0), (8, 2, 0, 3),
+    (8, 0, 1, 4), (4, 1, 1, 1), (5, 1, 1, 3), (6, 1, 1, 1), (8, 3, 1, 2), (6, 3, 1, 1), (8, 3, 0, 2), (7, 5),
+    (8, 5, 1, 1), (8, 5, 0, 1), (8, 2, 1, 4), (7, 4), (8, 4, 1, 1), (8, 4, 0, 1), (6, 2, 1, 1), (9, 0), (0, 2),
+    (8, 3, 1, 3), (8, 3, 0, 3), (7, 6), (8, 6, 1, 1), (8, 5, 0, 2), (8, 6, 0, 1), (8, 5, 1, 2), (9, 2), (8, 4, 0, 2),
+    (8, 4, 1, 2), (1,), (8, 3, 0, 4), (8, 6, 1, 2), (8, 5, 0, 3), (8, 5, 1, 3), (8, 6, 0, 2), (8, 4, 1, 3), (10, 0),
+    (10, 1), (9, 3), (8, 5, 0, 4), (8, 4, 0, 3), (8, 6, 1, 3), (10, 2), (8, 6, 0, 3), (8, 4, 1, 4), (13, 7), (9, 5),
+    (11, 1, 0, 2), (11, 0, 0, 2), (8, 6, 1, 4), (11, 0, 1, 2), (11, 2, 1, 2), (11, 2, 0, 2), (9, 4), (11, 7, 0, 2),
+    (11, 7, 1, 2), (10, 3), (11, 0, 1, 3), (11, 0, 0, 3), (9, 6), (11, 2, 1, 3), (11, 2, 0, 3), (11, 7, 0, 3),
+    (10, 5), (11, 3, 0, 2), (11, 1, 1, 2), (11, 0, 1, 4), (11, 3, 1, 2), (11, 1, 0, 3), (10, 4), (11, 7, 1, 3),
+    (11, 7, 0, 4), (11, 5, 1, 2), (11, 5, 0, 2), (11, 3, 0, 3), (10, 6), (11, 2, 1, 4), (11, 1, 0, 4), (11, 4, 1, 2),
+    (12, 0), (11, 5, 0, 3), (11, 4, 0, 2), (11, 6, 1, 2), (11, 5, 1, 3), (11, 6, 0, 2), (11, 3, 0, 4), (11, 4, 1, 3),
+    (12, 7), (11, 6, 1, 3), (11, 3, 1, 3), (11, 1, 1, 3), (11, 5, 0, 4), (11, 4, 0, 3), (11, 4, 1, 4), (11, 6, 0, 3),
+    (11, 6, 1, 4), (12, 2), (12, 5), (12, 3), (12, 1), (12, 4), (12, 6),
 )
 
 
@@ -87,6 +87,9 @@
     def xcdev(j):
         t = rem(xc + j, 2 * NX)
         return dev(div(t, 2), y, z, rem(t, 2))
+
+    def mirror(j, dy, dc):
+        return dev(rem(x + j, NX), rem(y + dy * NY, 2 * NY), z, c if dc == 0 else 1 - c)
 
     sibling = dev(x, y, z, 1 - c)
     tile_next = (rem(e + 1, NZ * NY), o)
@@ -273,9 +276,10 @@
     def pair(g):
         return pl.ds(slots(g)[0], PAIR)
 
-    rs_id = [[[ids() for s in range(hops(g)[d])] for d in range(2)] for g in range(GROUPS)]
+    rs_id = [[[ids() for s in range(hops(g)[d])] for d in range(2)] for g in range(SUMMED)]
     ag_id = [[[ids() for s in range(hops(g)[d])] for d in range(2)] for g in range(GROUPS)]
-    y_id = [[ids() for j in range(NY - 1)] for g in range(GROUPS)]
+    y_id = [[ids() for j in range(NY - 1)] for g in range(SUMMED)]
+    mir_id = [[ids() for dc in range(PAIR)]]
 
     def along_z(d):
         return zdev(1 if d == 0 else NZ - 1)
@@ -325,6 +329,18 @@
         tfull[pair(g), strip(z), :] = value.astype(BF16)
         for d in range(2):
             ag_send(g, d, 1)
+        dx, dy = members[g]
+        if (dx, dy) == (1, 0):
+            for dc in range(PAIR):
+                push(tfull.at[slot_of(1, dy, dc), strip(z), :], tfull.at[slot_of(3, dy, dc), strip(z), :],
+                     mir_id[dy][dc], mirror(1, dy, dc))
+
+    def do_mir(g):
+        dx, dy = members[g]
+        for dc in range(PAIR):
+            arrived(tfull.at[slot_of(3, dy, dc), strip(z), :], mir_id[dy][dc])
+        for d in range(2):
+            ag_send(g, d, 1)
 
     do_ag = ag_send
 
@@ -334,13 +350,16 @@
             arrived(region(g, rem(z + (NZ - n if d == 0 else n), NZ)), ag_id[g][d][n - 1])
         initial, final = g == mixes[0], g == mixes[-1]
 
-        def step(t, carry):
-            rows = pl.ds(pl.multiple_of(t * 256, 256), 256)
-            value = None
-            for q in slots(g):
-                term = lax.dot_general(
-                    panel[q, rows, :], tfull[q], (((1,), (1,)), ((), ())), preferred_element_type=F32)
-                value = term if value is None else value + term
+        mirrored = members[g] == (3, 0)
+        if mirrored:
+            for h in range(2):
+                from_sibling(*members[g], h)
+        side = 0 if mirrored else 1
+        strips = jnp.concatenate([tfull[q] for q in slots(g)], axis=side)
+        for t in range(ROWS // MIX_ROWS):
+            rows = pl.ds(t * MIX_ROWS, MIX_ROWS)
+            left = jnp.concatenate([panel[q, rows, :] for q in slots(g)], axis=1)
+            value = lax.dot_general(left, strips, (((1,), (side,)), ((), ())), preferred_element_type=F32)
             if not initial:
                 value = value + mixed[rows, :]
             if final:
@@ -348,8 +367,6 @@
                 out_ref[rows, :] = ((1.5 * f - 0.5 * value) / jnp.max(lev[1])).astype(BF16)
             else:
                 mixed[rows, :] = value
-            return carry
-        lax.fori_loop(0, ROWS // 256, step, 0)
 
     def transposed(h):
         ft[pl.ds(h * HALF, HALF), :] = panel[0, :, cols(h)].T
@@ -378,7 +395,7 @@
             else:
                 launch(h)
 
-    steps = (do_ls, do_ld, do_yr, do_par, do_f3, do_f1, do_sib, do_gram, do_rs, do_rsd, do_sc, do_ag, do_mix)
+    steps = (do_ls, do_ld, do_yr, do_par, do_f3, do_f1, do_sib, do_gram, do_rs, do_rsd, do_sc, do_ag, do_mix, do_mir)
     mixes = [numbers[0] for kind, *numbers in ORDER if steps[kind] is do_mix]
     for kind, *numbers in ORDER:
         steps[kind](*numbers)

time: 117 us -> 116 us (level)
  no operation moved by 1% of the time
where the time goes in v3:
time: 116 us
  Pallas kernels  114 us (98%)
  local copies, waits for them, and re-layouts  1.77 us (2%)
    pallas_call x1, Pallas kernels, local(): pl.pallas_call(lambda *refs: kernel(total_rows, total_cols, *refs), out_s...  114 us

profile of v3, /device:TPU:6, one launch (start us, length us, event | category | flops | bytes accessed | tf_op | source)
XLA Modules:
  0.0 115.9 jit_solution(9852292745905407706)
XLA Ops:
  0.0 114.1 %filter_gram.1 = bf16[768,256]{1,0:T(8,128)(2,1)} custom-call(bf16[12,64,256]{2,1,0:T(8,128)(2,1)} %bitcast.2, bf16[12,7,64,64]{3,2,1,0:T(8,128)(2,1)} %refs_1_.1, s32[7,12]{1,0:T(8,128)} %bitcast.3), custom_call_target="tpu_custom_call" | custom-call | tf_op jit(solution)/shard_map/filter_gram/pallas_call | solution.py:416
  114.1 1.8 %copy.5 = bf16[768,256]{1,0:T(8,128)(2,1)} copy(bf16[768,256]{1,0:T(8,128)(2,1)} %filter_gram.1) | data formatting | bytes 786432

commit v4 on v3

--- a/solution.py
+++ b/solution.py
@@ -23,26 +23,26 @@
 N_SEND, N_RECV = 256, 256
 members = ((1, 0), (0, 0), (2, 0), (0, 1), (3, 1), (1, 1), (2, 1), (3, 0))
 ORDER = (
-    (0, 0), (7, 1), (4, 0, 0, 1), (8, 1, 0, 1), (5, 0, 0, 2), (5, 0, 0, 3), (4, 0, 0, 0), (2, 0, 0), (6, 1, 0, 0),
-    (6, 3, 0, 0), (2, 0, 2), (8, 1, 1, 1), (2, 0, 1), (2, 0, 3), (5, 0, 1, 2), (4, 0, 1, 0), (8, 1, 0, 2), (2, 1, 2),
-    (8, 1, 1, 2), (2, 1, 0), (5, 0, 1, 3), (4, 0, 1, 1), (6, 1, 0, 1), (2, 1, 1), (3, 0, 0), (6, 3, 0, 1), (2, 1, 3),
-    (6, 2, 0, 0), (7, 0), (8, 0, 1, 1), (8, 0, 0, 1), (3, 0, 2), (3, 0, 1), (8, 1, 0, 3), (6, 2, 0, 1), (0, 1),
-    (8, 1, 1, 3), (3, 0, 3), (8, 0, 0, 2), (8, 0, 1, 2), (6, 0, 1, 0), (5, 1, 0, 2), (4, 1, 0, 0), (7, 2),
-    (8, 2, 1, 1), (3, 1, 0), (8, 2, 0, 1), (3, 1, 2), (4, 1, 0, 1), (5, 1, 0, 3), (3, 1, 1), (6, 1, 1, 0),
-    (8, 1, 0, 4), (3, 1, 3), (6, 0, 1, 1), (8, 0, 1, 3), (6, 3, 1, 0), (8, 0, 0, 3), (8, 2, 1, 2), (8, 2, 0, 2),
-    (7, 3), (4, 1, 1, 0), (8, 3, 0, 1), (5, 1, 1, 2), (8, 3, 1, 1), (8, 2, 1, 3), (9, 1), (6, 2, 1, 0), (8, 2, 0, 3),
-    (8, 0, 1, 4), (4, 1, 1, 1), (5, 1, 1, 3), (6, 1, 1, 1), (8, 3, 1, 2), (6, 3, 1, 1), (8, 3, 0, 2), (7, 5),
-    (8, 5, 1, 1), (8, 5, 0, 1), (8, 2, 1, 4), (7, 4), (8, 4, 1, 1), (8, 4, 0, 1), (6, 2, 1, 1), (9, 0), (0, 2),
-    (8, 3, 1, 3), (8, 3, 0, 3), (7, 6), (8, 6, 1, 1), (8, 5, 0, 2), (8, 6, 0, 1), (8, 5, 1, 2), (9, 2), (8, 4, 0, 2),
-    (8, 4, 1, 2), (1,), (8, 3, 0, 4), (8, 6, 1, 2), (8, 5, 0, 3), (8, 5, 1, 3), (8, 6, 0, 2), (8, 4, 1, 3), (10, 0),
-    (10, 1), (9, 3), (8, 5, 0, 4), (8, 4, 0, 3), (8, 6, 1, 3), (10, 2), (8, 6, 0, 3), (8, 4, 1, 4), (13, 7), (9, 5),
-    (11, 1, 0, 2), (11, 0, 0, 2), (8, 6, 1, 4), (11, 0, 1, 2), (11, 2, 1, 2), (11, 2, 0, 2), (9, 4), (11, 7, 0, 2),
-    (11, 7, 1, 2), (10, 3), (11, 0, 1, 3), (11, 0, 0, 3), (9, 6), (11, 2, 1, 3), (11, 2, 0, 3), (11, 7, 0, 3),
-    (10, 5), (11, 3, 0, 2), (11, 1, 1, 2), (11, 0, 1, 4), (11, 3, 1, 2), (11, 1, 0, 3), (10, 4), (11, 7, 1, 3),
-    (11, 7, 0, 4), (11, 5, 1, 2), (11, 5, 0, 2), (11, 3, 0, 3), (10, 6), (11, 2, 1, 4), (11, 1, 0, 4), (11, 4, 1, 2),
-    (12, 0), (11, 5, 0, 3), (11, 4, 0, 2), (11, 6, 1, 2), (11, 5, 1, 3), (11, 6, 0, 2), (11, 3, 0, 4), (11, 4, 1, 3),
-    (12, 7), (11, 6, 1, 3), (11, 3, 1, 3), (11, 1, 1, 3), (11, 5, 0, 4), (11, 4, 0, 3), (11, 4, 1, 4), (11, 6, 0, 3),
-    (11, 6, 1, 4), (12, 2), (12, 5), (12, 3), (12, 1), (12, 4), (12, 6),
+    (5, 0, 0, 3), (2, 0, 2), (2, 0, 0), (7, 1), (4, 0, 0, 0), (5, 0, 0, 2), (8, 1, 1, 1), (4, 0, 0, 1), (8, 1, 0, 1),
+    (4, 0, 1, 0), (4, 0, 1, 1), (2, 0, 3), (2, 0, 1), (5, 0, 1, 2), (8, 1, 0, 2), (6, 1, 0, 0), (2, 1, 1), (0, 0),
+    (2, 1, 0), (8, 1, 1, 2), (5, 0, 1, 3), (6, 1, 0, 1), (2, 1, 2), (3, 0, 0), (2, 1, 3), (7, 0), (8, 0, 1, 1),
+    (8, 1, 0, 3), (8, 0, 0, 1), (3, 0, 2), (6, 2, 0, 0), (3, 0, 1), (6, 2, 0, 1), (8, 1, 1, 3), (3, 0, 3),
+    (8, 0, 1, 2), (8, 1, 0, 4), (3, 1, 1), (7, 2), (8, 0, 0, 2), (6, 0, 1, 0), (8, 2, 1, 1), (0, 1), (8, 2, 0, 1),
+    (3, 1, 2), (3, 1, 0), (3, 1, 3), (6, 0, 1, 1), (4, 1, 0, 0), (5, 1, 0, 3), (8, 0, 1, 3), (8, 2, 1, 2),
+    (4, 1, 0, 1), (9, 1), (7, 3), (8, 3, 0, 1), (8, 2, 0, 2), (8, 0, 0, 3), (4, 1, 1, 0), (5, 1, 1, 2), (5, 1, 0, 2),
+    (6, 1, 1, 0), (4, 1, 1, 1), (8, 3, 1, 1), (6, 3, 1, 0), (5, 1, 1, 3), (6, 1, 1, 1), (8, 0, 1, 4), (6, 3, 1, 1),
+    (8, 2, 1, 3), (8, 3, 0, 2), (7, 5), (8, 5, 0, 1), (6, 3, 0, 1), (8, 5, 1, 1), (7, 4), (8, 2, 0, 3), (8, 3, 1, 2),
+    (0, 2), (9, 0), (8, 4, 0, 1), (6, 2, 1, 0), (8, 4, 1, 1), (8, 3, 0, 3), (8, 2, 1, 4), (6, 2, 1, 1), (8, 5, 0, 2),
+    (8, 5, 1, 2), (7, 6), (8, 6, 1, 1), (8, 6, 0, 1), (1,), (8, 3, 1, 3), (10, 1), (9, 2), (8, 3, 0, 4), (8, 4, 1, 2),
+    (8, 5, 0, 3), (8, 4, 0, 2), (8, 6, 1, 2), (8, 5, 1, 3), (10, 0), (11, 1, 0, 2), (9, 3), (8, 5, 0, 4),
+    (8, 6, 0, 2), (8, 4, 1, 3), (11, 1, 1, 2), (8, 6, 1, 3), (8, 4, 0, 3), (11, 1, 0, 3), (8, 4, 1, 4), (13, 7),
+    (9, 5), (10, 2), (11, 0, 0, 2), (8, 6, 1, 4), (8, 6, 0, 3), (11, 0, 1, 2), (10, 3), (9, 4), (11, 7, 1, 2),
+    (11, 0, 0, 3), (11, 7, 0, 2), (6, 3, 0, 0), (11, 2, 1, 2), (9, 6), (11, 1, 0, 4), (11, 1, 1, 3), (11, 0, 1, 3),
+    (10, 5), (11, 2, 0, 2), (11, 3, 1, 2), (11, 7, 1, 3), (11, 3, 0, 2), (11, 7, 0, 3), (11, 2, 1, 3), (10, 4),
+    (11, 5, 0, 2), (11, 0, 1, 4), (11, 3, 0, 3), (10, 6), (11, 5, 1, 2), (11, 4, 1, 2), (11, 3, 1, 3), (11, 5, 0, 3),
+    (11, 4, 0, 2), (11, 7, 0, 4), (11, 6, 1, 2), (11, 2, 0, 3), (11, 6, 0, 2), (11, 2, 1, 4), (11, 4, 1, 3),
+    (11, 3, 0, 4), (11, 5, 0, 4), (11, 6, 1, 3), (11, 4, 0, 3), (11, 5, 1, 3), (12, 1), (11, 4, 1, 4), (12, 7),
+    (11, 6, 0, 3), (11, 6, 1, 4), (12, 0), (12, 2), (12, 3), (12, 5), (12, 4), (12, 6),
 )
 
 

time: 116 us -> 115 us (level); the launches traced: 116 us -> 113 us
  Pallas kernels: 114 us -> 111 us
    pallas_call x1, Pallas kernels: 114 us -> 111 us  [local(): pl.pallas_call(lambda *refs: kernel(total_rows, total_cols, *refs), out_s...]
where the time goes in v4:
time: 115 us; the launch traced here: 113 us
  Pallas kernels  111 us (97%)
  local copies, waits for them, and re-layouts  1.77 us (2%)
    pallas_call x1, Pallas kernels, local(): pl.pallas_call(lambda *refs: kernel(total_rows, total_cols, *refs), out_s...  111 us

profile of v4, /device:TPU:6, one launch (start us, length us, event | category | flops | bytes accessed | tf_op | source)
XLA Modules:
  0.0 112.7 jit_solution(4781706343787448059)
XLA Ops:
  0.0 111.0 %filter_gram.1 = bf16[768,256]{1,0:T(8,128)(2,1)} custom-call(bf16[12,64,256]{2,1,0:T(8,128)(2,1)} %bitcast.2, bf16[12,7,64,64]{3,2,1,0:T(8,128)(2,1)} %refs_1_.1, s32[7,12]{1,0:T(8,128)} %bitcast.3), custom_call_target="tpu_custom_call" | custom-call | tf_op jit(solution)/shard_map/filter_gram/pallas_call | solution.py:416
  111.0 1.8 %copy.5 = bf16[768,256]{1,0:T(8,128)(2,1)} copy(bf16[768,256]{1,0:T(8,128)(2,1)} %filter_gram.1) | data formatting | bytes 786432

commit v5 on v4

--- a/solution.py
+++ b/solution.py
@@ -262,7 +262,7 @@
         total = jnp.sum(jnp.sum(lx[...], axis=0))
         level = jnp.full((8, HALF), total) / (total_cols * total_rows)
         lev[0] = level * total_rows
-        lev[1] = jnp.sqrt(level)
+        lev[1] = 1.0 / jnp.sqrt(level)
 
     def slots(g):
         return [slot_of(*members[g], dc) for dc in range(PAIR)]
@@ -364,7 +364,7 @@
                 value = value + mixed[rows, :]
             if final:
                 f = panel[0, rows, :].astype(F32)
-                out_ref[rows, :] = ((1.5 * f - 0.5 * value) / jnp.max(lev[1])).astype(BF16)
+                out_ref[rows, :] = ((1.5 * f - 0.5 * value) * jnp.max(lev[1])).astype(BF16)
             else:
                 mixed[rows, :] = value
 
@@ -397,7 +397,14 @@
 
     steps = (do_ls, do_ld, do_yr, do_par, do_f3, do_f1, do_sib, do_gram, do_rs, do_rsd, do_sc, do_ag, do_mix, do_mir)
     mixes = [numbers[0] for kind, *numbers in ORDER if steps[kind] is do_mix]
-    for kind, *numbers in ORDER:
+    settled = 0
+    for n, (kind, *numbers) in enumerate(ORDER):
+        if n == len(ORDER) - 40:
+            settled = len(finals)
+        if n == len(ORDER) - 1:
+            for fn in finals[:settled]:
+                fn()
+            del finals[:settled]
         steps[kind](*numbers)
     for fn in finals:
         fn()

time: 115 us -> 115 us (level)
  no operation moved by 1% of the time
where the time goes in v5:
time: 115 us; the launch traced here: 112 us
  Pallas kernels  111 us (97%)
  local copies, waits for them, and re-layouts  1.77 us (2%)
    pallas_call x1, Pallas kernels, local(): pl.pallas_call(lambda *refs: kernel(total_rows, total_cols, *refs), out_s...  111 us

profile of v5, /device:TPU:6, one launch (start us, length us, event | category | flops | bytes accessed | tf_op | source)
XLA Modules:
  0.0 112.4 jit_solution(17421198644453638892)
XLA Ops:
  0.0 110.7 %filter_gram.1 = bf16[768,256]{1,0:T(8,128)(2,1)} custom-call(bf16[12,64,256]{2,1,0:T(8,128)(2,1)} %bitcast.2, bf16[12,7,64,64]{3,2,1,0:T(8,128)(2,1)} %refs_1_.1, s32[7,12]{1,0:T(8,128)} %bitcast.3), custom_call_target="tpu_custom_call" | custom-call | tf_op jit(solution)/shard_map/filter_gram/pallas_call | solution.py:423
  110.7 1.8 %copy.5 = bf16[768,256]{1,0:T(8,128)(2,1)} copy(bf16[768,256]{1,0:T(8,128)(2,1)} %filter_gram.1) | data formatting | bytes 786432
